TPU v7x, 32 devices: a whole 2x2x4 slice. The times are simulated.
32 devices in a mesh: grp: 2 (over y), tile: 4 (over x, core), tp: 4 (over z).
Axes of the slice: x: 2, y: 2, z: 4, core: 2. Of those that a mesh axis runs over, the one named last changes fastest.
Arguments:
- atmos_state: bfloat16 [4096, 1536], P(('grp', 'tile')), may hold values from -6 to 6
- atmos_gain: float32 [1536], replicated, may hold values from 0.25 to 1.75
- w_first: bfloat16 [1536, 3072], P(('grp', 'tile'), 'tp'), may hold values from -0.15625 to 0.15625
- w_second: bfloat16 [1536, 3072], P(('grp', 'tile'), 'tp'), may hold values from -0.109375 to 0.109375
- flux_proj: bfloat16 [1536, 256], replicated, may hold values from -0.15625 to 0.15625
- remap_index: int32 [64, 3], P(('grp', 'tile', 'tp')), may hold values from 0 to 3
- remap_weight: bfloat16 [64, 3, 128, 128], P(('grp', 'tile', 'tp')), may hold values from -0.3125 to 0.3125
- ocean_state: bfloat16 [64, 128, 256], P(('grp', 'tile'), 'tp'), may hold values from -6 to 6
- depth_levels: int32 [64, 128], P(('grp', 'tile'), 'tp'), may hold values from 0 to 16
- conv_kernel: float32 [3, 3, 256], replicated, may hold values from -2 to 2
- ocean_gain: float32 [256], replicated, may hold values from 0.25 to 1.75
- ocean_w_in: bfloat16 [256, 1024], replicated, may hold values from -0.375 to 0.375
- ocean_w_out: bfloat16 [1024, 256], replicated, may hold values from -0.1875 to 0.1875
- ocean_cotangent: bfloat16 [64, 128, 256], P(('grp', 'tile'), 'tp'), may hold values from -6 to 6
Outputs:
- atmos_out: bfloat16 [4096, 1536], P(('grp', 'tile', 'tp'))
- ocean_out: bfloat16 [64, 128, 256], P(('grp', 'tile'), 'tp')
- weight_grads: float32 [2048, 256], P(('grp', 'tile', 'tp'))
Inputs may be any that keep to these rules, and one draw needn't show every extreme that they name: `remap_index`: index the 128-token blocks among the 512 atmosphere tokens of the same grp and tile indices as the ocean tile of that block. `depth_levels`: 0 marks land.
All inputs are finite; a program needn't handle non-finite values.
Results may differ from a plain program's by a relative error of at most 0.018.
Values may be sent and summed in bfloat16 or wider, within the bound.
No kernel may reach another device: no remote copies, remote signals or barrier semaphores. Data moves between devices by JAX's collectives and lax.ppermute only.
A program may use at most 64 MiB of HBM per device.

v0:
```python
import jax
import jax.numpy as jnp
from jax import lax
from jax.sharding import PartitionSpec as P

LEV = 16
epsilon = 1e-06


def with_halo(block, sides, width):
    for axis, dim in sides:
        count = lax.axis_size(axis)
        forward = [(i, i + 1) for i in range(count - 1)]
        backward = [(target, source) for source, target in forward]
        low = lax.ppermute(
            lax.slice_in_dim(block, block.shape[dim] - width, None, axis=dim), axis, forward
        )
        high = lax.ppermute(lax.slice_in_dim(block, 0, width, axis=dim), axis, backward)
        block = jnp.concatenate([low, block, high], axis=dim)
    return block


def rms_norm(values, gain):
    wide = values.astype(jnp.float32)
    scale = lax.rsqrt(jnp.mean(wide * wide, axis=-1, keepdims=True) + epsilon)
    return (wide * scale * gain).astype(jnp.bfloat16)


def on_device(
    atmos_state,
    atmos_gain,
    w_first,
    w_second,
    flux_proj,
    remap_index,
    remap_weight,
    ocean_state,
    depth_levels,
    conv_kernel,
    ocean_gain,
    ocean_w_in,
    ocean_w_out,
    ocean_cotangent,
):
    normed = rms_norm(atmos_state, atmos_gain)
    rows_all = atmos_state.shape[0]
    hsum = jnp.dot(
        normed,
        lax.all_gather(w_first, ("grp", "tile"), axis=0, tiled=True),
        preferred_element_type=jnp.float32,
    )
    hidden = jax.nn.gelu(hsum).astype(jnp.bfloat16)
    partial_sum = lax.dot_general(
        hidden,
        lax.all_gather(w_second, ("grp", "tile"), axis=0, tiled=True),
        (((1,), (1,)), ((), ())),
        preferred_element_type=jnp.float32,
    )
    rows_own = rows_all // lax.axis_size("tp")
    block_rows = remap_weight.shape[2]
    channels = flux_proj.shape[1]
    summed = lax.psum_scatter(
        partial_sum.astype(jnp.bfloat16), "tp", scatter_dimension=0, tiled=True
    ).astype(jnp.float32)
    own_rows = lax.dynamic_slice_in_dim(atmos_state, lax.axis_index("tp") * rows_own, rows_own, 0)
    atmos_out = (own_rows.astype(jnp.float32) + summed).astype(jnp.bfloat16)
    flux = jnp.dot(atmos_out, flux_proj, preferred_element_type=jnp.float32).astype(jnp.bfloat16)
    piece = lax.all_gather(flux, "tp", axis=0, tiled=True)
    count = piece.shape[0] // block_rows
    blocks = piece.reshape(count, block_rows, channels)
    targets = jnp.arange(count, dtype=jnp.int32)
    select = (remap_index[:, :, None] == targets[None, None, :]).astype(jnp.bfloat16)
    picked = jnp.einsum("bkj,jrc->bkrc", select, blocks, preferred_element_type=jnp.float32).astype(
        jnp.bfloat16
    )
    remapped = jnp.einsum(
        "bksr,bkrc->bsc", remap_weight, picked, preferred_element_type=jnp.float32
    )
    tile_x, tile_y, _ = ocean_state.shape
    levels = jnp.arange(channels, dtype=jnp.int32) // (channels // LEV)
    wet = (levels[None, None, :] < depth_levels[:, :, None]).astype(jnp.float32)
    moved = remapped.astype(jnp.bfloat16).reshape(tile_x, tile_y, channels)
    field = ((ocean_state.astype(jnp.float32) + moved.astype(jnp.float32)) * wet).astype(
        jnp.bfloat16
    )
    padded = with_halo(field, ((("grp", "tile"), 0), ("tp", 1)), 1).astype(jnp.float32)
    conv = jnp.zeros((tile_x, tile_y, channels), jnp.float32)
    for i in range(3):
        for j in range(3):
            conv = conv + conv_kernel[i, j] * padded[i : i + tile_x, j : j + tile_y]
    centred = conv - jnp.mean(conv, axis=-1, keepdims=True)
    variance = jnp.mean(centred * centred, axis=-1, keepdims=True)
    cells = tile_x * tile_y
    ocean_normed = (
        (centred * lax.rsqrt(variance + epsilon) * ocean_gain)
        .astype(jnp.bfloat16)
        .reshape(cells, channels)
    )
    flat_field = field.reshape(cells, channels)
    flat_wet = wet.reshape(cells, channels)
    pre = jnp.dot(ocean_normed, ocean_w_in, preferred_element_type=jnp.float32)
    activated, backward = jax.vjp(jax.nn.gelu, pre)
    activated = activated.astype(jnp.bfloat16)
    out = jnp.dot(activated, ocean_w_out, preferred_element_type=jnp.float32)
    ocean_out = (
        ((flat_field.astype(jnp.float32) + out) * flat_wet)
        .astype(jnp.bfloat16)
        .reshape(tile_x, tile_y, channels)
    )
    dout = (ocean_cotangent.reshape(cells, channels).astype(jnp.float32) * flat_wet).astype(
        jnp.bfloat16
    )
    dact = lax.dot_general(
        dout, ocean_w_out, (((1,), (1,)), ((), ())), preferred_element_type=jnp.float32
    )
    dpre = backward(dact)[0].astype(jnp.bfloat16)
    grad_in = lax.dot_general(
        dpre, ocean_normed, (((0,), (0,)), ((), ())), preferred_element_type=jnp.float32
    )
    grad_out = lax.dot_general(
        activated, dout, (((0,), (0,)), ((), ())), preferred_element_type=jnp.float32
    )
    terms = jnp.concatenate([grad_in, grad_out], axis=0)
    weight_grads = lax.psum_scatter(terms, ("grp", "tile", "tp"), scatter_dimension=0, tiled=True)
    return (atmos_out, ocean_out, weight_grads)


def solution(mesh):
    in_specs = (
        P(("grp", "tile"), None),
        P(),
        P(("grp", "tile"), "tp"),
        P(("grp", "tile"), "tp"),
        P(),
        P(("grp", "tile", "tp"), None),
        P(("grp", "tile", "tp"), None, None, None),
        P(("grp", "tile"), "tp", None),
        P(("grp", "tile"), "tp"),
        P(),
        P(),
        P(),
        P(),
        P(("grp", "tile"), "tp", None),
    )
    out_specs = (
        P(("grp", "tile", "tp"), None),
        P(("grp", "tile"), "tp", None),
        P(("grp", "tile", "tp"), None),
    )
    return jax.shard_map(
        on_device, mesh=mesh, in_specs=in_specs, out_specs=out_specs, check_vma=False
    )
```

profile of v0, /device:TPU:0, one launch (start us, length us, event | category | flops | bytes accessed | tf_op | source)
XLA Modules:
  0.0 300.5 jit_solution(9202283299108384426)
XLA Ops:
  7.2 0.7 all-gather.5.cloned.1.call-update
  8.0 0.7 all-gather.3.cloned.1.call-update
  8.7 1.8 fusion
  10.5 31.0 %all-gather.5.cloned.1.call-done = bf16[1536,768]{1,0:T(8,128)(2,1)} async-done(((bf16[192,768]{1,0:T(8,128)(2,1)}), bf16[1536,768]{1,0:T(8,128)(2,1)}) %all-gather.5.cloned.1.call-update) | async-done | bytes 2359312 | tf_op jit(solution)/shard_map/all_gather | solution.py:55
  41.5 30.8 %all-gather.3.cloned.1.call-done = bf16[1536,768]{1,0:T(8,128)(2,1)} async-done(((bf16[192,768]{1,0:T(8,128)(2,1)}), bf16[1536,768]{1,0:T(8,128)(2,1)}) %all-gather.3.cloned.1.call-update) | async-done | bytes 2359312 | tf_op jit(solution)/shard_map/all_gather | solution.py:49
  72.3 6.9 %convolution_convert_fusion = bf16[512,1536]{1,0:T(8,128)(2,1)} fusion(bf16[1536,768]{1,0:T(8,128)(2,1)} %all-gather.5.cloned.1.call-done, bf16[1536,768]{1,0:T(8,128)(2,1)} %all-gather.3.cloned.1.call-done, bf16[512,1536]{1,0:T(8,128)(2,1)S(1)} %copy-done.1, f32[1536]{0:T(1024)S(1)} %copy-done.12, f32[512]{0:T(512)S(1)} %add_rsqrt_fusion.1), kind=kOutput, calls=%fused_computation.5 | convolution fusion | flops 2423390208 | bytes 7872512 | tf_op jit(solution)/shard_map/dot_general | solution.py:53
  79.3 0.6 copy-done.7
  80.0 34.8 %reduce-scatter.3.cloned.1.call-done = bf16[128,1536]{1,0:T(8,128)(2,1)} async-done(((bf16[512,1536]{1,0:T(8,128)(2,1)}), bf16[128,1536]{1,0:T(8,128)(2,1)}) %reduce-scatter.3.cloned.1.call-update) | async-done | bytes 393232 | tf_op jit(solution)/shard_map/reduce_scatter | solution.py:62
  114.8 1.1 add_convert_fusion
  116.0 0.3 convolution_convert_fusion.1
  116.3 14.6 %all_gather.11 = bf16[512,256]{1,0:T(8,128)(2,1)S(1)} all-gather(bf16[128,256]{1,0:T(8,128)(2,1)S(1)} %convolution_convert_fusion.1), channel_id=1, replica_groups=mesh['grp'=2,'tile'=4,'tp'=4] {'tp'}, dimensions={0}, use_global_device_ids=true | all-gather | bytes 327680 | tf_op jit(solution)/shard_map/all_gather | solution.py:68
  130.8 0.4 fusion.41
  131.2 0.2 fusion.19
  131.5 0.1 select_convert_fusion
  131.6 1.3 collective-permute-start.1
  132.9 3.0 %collective-permute-start = (bf16[1,32,256]{2,1,0:T(8,128)(2,1)S(1)}, bf16[1,32,256]{2,1,0:T(8,128)(2,1)S(1)}, u32[]{:S(2)}, u32[]{:S(2)}) collective-permute-start(bf16[1,32,256]{2,1,0:T(8,128)(2,1)S(1)} %get-tuple-element.7), channel_id=1, source_target_pairs={{0,4},{4,8},{8,12},{12,16},{16,20},{20,24},{24,28},{1,5},{5,9},{9,... | collective-permute-start | bytes 49160 | tf_op jit(solution)/shard_map/ppermute | solution.py:15
  136.1 0.7 collective-permute-done
  136.8 1.3 collective-permute-start.3
  138.1 4.5 %collective-permute-start.2 = (bf16[10,1,256]{2,1,0:T(2,128)(2,1)S(1)}, bf16[10,1,256]{2,1,0:T(2,128)(2,1)S(1)}, u32[]{:S(2)}, u32[]{:S(2)}) collective-permute-start(bf16[10,1,256]{2,1,0:T(2,128)(2,1)S(1)} %get-tuple-element.5), channel_id=1, source_target_pairs={{0,1},{1,2},{2,3},{4,5},{5,6},{6,7},{8,9},{9,10},{10,11},{12,13},{... | collective-permute-start | bytes 15368 | tf_op jit(solution)/shard_map/ppermute | solution.py:15
  142.7 1.3 collective-permute-done.2
  144.1 0.3 fusion.57
  144.4 0.2 multiply_reduce_fusion
  144.6 0.2 copy-done.10
  144.8 0.1 multiply_convert_fusion.1
  144.9 0.2 copy-done.3
  145.1 0.3 fusion.63
  145.4 0.6 fusion.56
  146.0 3.1 %fusion.30 = f32[1024,256]{1,0:T(8,128)} fusion(bf16[256,256]{1,0:T(8,128)(2,1)S(1)} %bitcast.50, f32[256,1024]{1,0:T(8,128)S(1)} %fusion.63, bf16[256,256]{1,0:T(8,128)(2,1)S(1)} %fusion.32, bf16[1024,256]{1,0:T(8,128)(2,1)} %param.26), kind=kOutput, calls=%fused_computation.38 | convolution fusion | flops 273678336 | bytes 2883584 | tf_op jit(solution)/shard_map/dot_general | solution.py:117
  149.2 2.7 pad_maximum_fusion
  151.9 1.0 copy-done.11
  152.9 1.1 fusion.20
  154.0 139.9 %reduce-scatter.5.cloned.1.call-done = f32[64,256]{1,0:T(8,128)} async-done(((f32[2048,256]{1,0:T(8,128)}), f32[64,256]{1,0:T(8,128)}) %reduce-scatter.5.cloned.1.call-update) | async-done | bytes 65552 | tf_op jit(solution)/shard_map/reduce_scatter | solution.py:124
  (40 shorter events, 0.6 us)
Async XLA Ops:
  7.2 108.8 %copy-start = (bf16[1536,256]{1,0:T(8,128)(2,1)S(1)}, bf16[1536,256]{1,0:T(8,128)(2,1)}, u32[]{:S(2)}) copy-start(bf16[1536,256]{1,0:T(8,128)(2,1)} %param.18) | copy-start | bytes 2359300
  7.2 65.1 %copy-start.1 = (bf16[512,1536]{1,0:T(8,128)(2,1)S(1)}, bf16[512,1536]{1,0:T(8,128)(2,1)}, u32[]{:S(2)}) copy-start(bf16[512,1536]{1,0:T(8,128)(2,1)} %param.14) | copy-start | bytes 4718596
  7.2 65.1 %copy-start.12 = (f32[1536]{0:T(1024)S(1)}, f32[1536]{0:T(1024)}, u32[]{:S(2)}) copy-start(f32[1536]{0:T(1024)} %param.15) | copy-start | bytes 18436
  7.2 34.3 %all-gather.5.cloned.1.call-start = ((), (), s32[]{:S(2)}) async-start(), calls=%async_computation.3 | async-start | bytes 2654208 | tf_op jit(solution)/shard_map/all_gather | solution.py:55
  7.9 64.4 %all-gather.3.cloned.1.call-start = ((), (), s32[]{:S(2)}) async-start(), calls=%async_computation.2 | async-start | bytes 2654208 | tf_op jit(solution)/shard_map/all_gather | solution.py:49
  8.7 106.1 %reduce-scatter.3.cloned.1.call-start = ((), (), s32[]{:S(2)}) async-start(), calls=%async_computation.4 | async-start | bytes 1966080 | tf_op jit(solution)/shard_map/reduce_scatter | solution.py:62
  79.2 0.7 copy-start.7
  79.2 51.6 %copy-start.9 = (s32[2,3]{1,0:T(2,128)S(1)}, s32[2,3]{1,0:T(2,128)}, u32[]{:S(2)}) copy-start(s32[2,3]{1,0:T(2,128)} %param.19) | copy-start | bytes 76
  79.2 214.7 %reduce-scatter.5.cloned.1.call-start = ((), (), s32[]{:S(2)}) async-start(), calls=%async_computation.5 | async-start | bytes 2162688 | tf_op jit(solution)/shard_map/reduce_scatter | solution.py:124
  80.0 51.2 %copy-start.4 = (bf16[2,3,128,128]{3,2,1,0:T(8,128)(2,1)S(1)}, bf16[2,3,128,128]{3,2,1,0:T(8,128)(2,1)}, u32[]{:S(2)}) copy-start(bf16[2,3,128,128]{3,2,1,0:T(8,128)(2,1)} %param.20) | copy-start | bytes 589828
  115.9 15.5 %copy-start.2 = (bf16[128,1536]{1,0:T(8,128)(2,1)}, bf16[128,1536]{1,0:T(8,128)(2,1)S(1)}, u32[]{:S(2)}) copy-start(bf16[128,1536]{1,0:T(8,128)(2,1)S(1)} %add_convert_fusion) | copy-start | bytes 1179652
  115.9 15.5 %copy-start.6 = (bf16[8,32,256]{2,1,0:T(8,128)(2,1)S(1)}, bf16[8,32,256]{2,1,0:T(8,128)(2,1)}, u32[]{:S(2)}) copy-start(bf16[8,32,256]{2,1,0:T(8,128)(2,1)} %param.21) | copy-start | bytes 393220
  116.2 19.7 %copy-start.5 = (bf16[8,32,256]{2,1,0:T(8,128)(2,1)S(1)}, bf16[8,32,256]{2,1,0:T(8,128)(2,1)}, u32[]{:S(2)}) copy-start(bf16[8,32,256]{2,1,0:T(8,128)(2,1)} %param.27) | copy-start | bytes 393220
  116.3 26.4 %copy-start.8 = (f32[3,3,256]{2,1,0:T(4,128)S(1)}, f32[3,3,256]{2,1,0:T(4,128)}, u32[]{:S(2)}) copy-start(f32[3,3,256]{2,1,0:T(4,128)} %param.23) | copy-start | bytes 27652
  131.6 4.5 %collective-permute-start.1 = (bf16[1,32,256]{2,1,0:T(8,128)(2,1)S(1)}, bf16[1,32,256]{2,1,0:T(8,128)(2,1)S(1)}, u32[]{:S(2)}, u32[]{:S(2)}) collective-permute-start(bf16[1,32,256]{2,1,0:T(8,128)(2,1)S(1)} %get-tuple-element.8), channel_id=1, source_target_pairs={{4,0},{8,4},{12,8},{16,12},{20,16},{24,20},{28,24},{5,1},{9,5},{13... | collective-permute-start | bytes 49160 | tf_op jit(solution)/shard_map/ppermute | solution.py:18
  132.9 3.9 %collective-permute-start = (bf16[1,32,256]{2,1,0:T(8,128)(2,1)S(1)}, bf16[1,32,256]{2,1,0:T(8,128)(2,1)S(1)}, u32[]{:S(2)}, u32[]{:S(2)}) collective-permute-start(bf16[1,32,256]{2,1,0:T(8,128)(2,1)S(1)} %get-tuple-element.7), channel_id=1, source_target_pairs={{0,4},{4,8},{8,12},{12,16},{16,20},{20,24},{24,28},{1,5},{5,9},{9,... | collective-permute-start | bytes 49160 | tf_op jit(solution)/shard_map/ppermute | solution.py:15
  136.8 5.9 %collective-permute-start.3 = (bf16[10,1,256]{2,1,0:T(2,128)(2,1)S(1)}, bf16[10,1,256]{2,1,0:T(2,128)(2,1)S(1)}, u32[]{:S(2)}, u32[]{:S(2)}) collective-permute-start(bf16[10,1,256]{2,1,0:T(2,128)(2,1)S(1)} %get-tuple-element.6), channel_id=1, source_target_pairs={{1,0},{2,1},{3,2},{5,4},{6,5},{7,6},{9,8},{10,9},{11,10},{13,12},{... | collective-permute-start | bytes 15368 | tf_op jit(solution)/shard_map/ppermute | solution.py:18
  138.1 5.9 %collective-permute-start.2 = (bf16[10,1,256]{2,1,0:T(2,128)(2,1)S(1)}, bf16[10,1,256]{2,1,0:T(2,128)(2,1)S(1)}, u32[]{:S(2)}, u32[]{:S(2)}) collective-permute-start(bf16[10,1,256]{2,1,0:T(2,128)(2,1)S(1)} %get-tuple-element.5), channel_id=1, source_target_pairs={{0,1},{1,2},{2,3},{4,5},{5,6},{6,7},{8,9},{9,10},{10,11},{12,13},{... | collective-permute-start | bytes 15368 | tf_op jit(solution)/shard_map/ppermute | solution.py:15
  144.1 0.7 copy-start.10
  144.1 1.0 copy-start.3
  151.9 1.0 copy-start.11
Sparse Core Ops, SparseCore 0:
  9.9 31.5 all-gather.4
  43.4 28.8 all-gather.2
  79.3 35.4 reduce-scatter.2
  152.0 141.8 reduce-scatter.4
where the time goes:
time: 301 us; the launch traced here: 300 us
  waiting for transfers between devices  240 us (80%)
  blocking collectives  14.6 us (5%)
  between operations  14 us (5%)
  matrix products  12.9 us (4%)
  starting transfers between devices  10.3 us (3%)
  other arithmetic  6.51 us (2%)
    reduce_scatter x1, waiting for transfers between devices, on_device(): lax.psum_scatter(terms, ('grp', 'tile', 'tp'), scatter_dimension=0, tiled...  140 us
    reduce_scatter x1, waiting for transfers between devices, on_device(): lax.psum_scatter(partial_sum.astype(jnp.bfloat16), 'tp', scatter_dimensio...  34.8 us
    all_gather x1, waiting for transfers between devices, on_device(): lax.all_gather(w_second, ('grp', 'tile'), axis=0, tiled=True)  31 us
    all_gather x1, waiting for transfers between devices, on_device(): lax.all_gather(w_first, ('grp', 'tile'), axis=0, tiled=True)  30.8 us
    all_gather x1, blocking collectives, on_device(): piece = lax.all_gather(flux, 'tp', axis=0, tiled=True)  14.6 us
    ppermute x2, starting transfers between devices, with_halo(): lax.ppermute(lax.slice_in_dim(block, block.shape[dim] - width, None, axis...  7.58 us
    dot_general x1, matrix products, on_device(): lax.dot_general(hidden, lax.all_gather(w_second, ('grp', 'tile'), axis=0,...  6.86 us
  transfers between devices with their start and end apart: 8, of which 6 were waited for; matrix products, arithmetic and copies ran while one was open for 1% of the time, Pallas kernels for 0%

commit v1 on v0

--- a/solution.py
+++ b/solution.py
@@ -50,9 +50,36 @@
         preferred_element_type=jnp.float32,
     )
     hidden = jax.nn.gelu(hsum).astype(jnp.bfloat16)
+
+    def _state_pages(matrix, on_dim):
+        v_next, carry, aux = (
+            lax.axis_size(("grp", "tile")),
+            lax.axis_index(("grp", "tile")),
+            matrix.shape[on_dim],
+        )
+        copies = list(map(lambda num: (num, (num + 1) % v_next), range(v_next)))
+        row_list = list(map(lambda num: (num, (num - 1) % v_next), range(v_next)))
+        val2 = jnp.zeros(
+            (*matrix.shape[:on_dim], v_next * aux, *matrix.shape[on_dim + 1 :]), matrix.dtype
+        )
+        val2 = lax.dynamic_update_slice_in_dim(val2, matrix, carry * aux, axis=on_dim)
+        raw_out = newest = matrix
+        ready = v_next // 2
+        for d in tuple(range(1, ready + 1)):
+            raw_out = lax.ppermute(raw_out, ("grp", "tile"), copies)
+            val2 = lax.dynamic_update_slice_in_dim(
+                val2, raw_out, (carry - d) % v_next * aux, axis=on_dim
+            )
+            if d < v_next - ready:
+                newest = lax.ppermute(newest, ("grp", "tile"), row_list)
+                val2 = lax.dynamic_update_slice_in_dim(
+                    val2, newest, (carry + d) % v_next * aux, axis=on_dim
+                )
+        return val2
+
     partial_sum = lax.dot_general(
         hidden,
-        lax.all_gather(w_second, ("grp", "tile"), axis=0, tiled=True),
+        _state_pages(w_second, 0),
         (((1,), (1,)), ((), ())),
         preferred_element_type=jnp.float32,
     )

time: 301 us -> 283 us (0.940)
  waiting for transfers between devices: 240 us -> 199 us
  starting transfers between devices: 10.3 us -> 25.8 us
  local copies, waits for them, and re-layouts: 2.17 us -> 8.64 us
    all_gather x1 -> x0, waiting for transfers between devices: 31 us -> none  [on_device(): lax.all_gather(w_second, ('grp', 'tile'), axis=0, tiled=True)]
    all_gather x1, waiting for transfers between devices: 30.8 us -> 1.65 us  [on_device(): lax.all_gather(w_first, ('grp', 'tile'), axis=0, tiled=True)]
    ppermute x0 -> x7, starting transfers between devices: none -> 17.1 us  [the longest x4 9.26 us: _state_pages(): raw_out = lax.ppermute(raw_out, ('grp', 'tile'), copies)]
    ppermute x0 -> x7, waiting for transfers between devices: none -> 12.8 us  [the longest x4 8.02 us: _state_pages(): raw_out = lax.ppermute(raw_out, ('grp', 'tile'), copies)]
    dynamic_update_slice x0 -> x8, local copies, waits for them, and re-layouts: none -> 6.88 us  [the longest x4 3.95 us: _state_pages(): lax.dynamic_update_slice_in_dim(val2, raw_out, (carry - d) % v_next * aux...]
    reduce_scatter x1, waiting for transfers between devices: 34.8 us -> 40.7 us  [on_device(): lax.psum_scatter(partial_sum.astype(jnp.bfloat16), 'tp', scatter_dimensio...]
    ppermute x2, waiting for transfers between devices: 0.01 us -> 3.36 us  [with_halo(): lax.ppermute(lax.slice_in_dim(block, 0, width, axis=dim), axis, backward)]
  transfers between devices with their start and end apart: 8 -> 14, of which waited for: 6 -> 10; matrix products, arithmetic and copies ran while one was open for 1% -> 4% of each run, Pallas kernels for 0% -> 0%
where the time goes in v1:
time: 283 us
  waiting for transfers between devices  199 us (70%)
  starting transfers between devices  25.8 us (9%)
  blocking collectives  14.4 us (5%)
  between operations  14 us (5%)
  matrix products  13.9 us (5%)
  local copies, waits for them, and re-layouts  8.64 us (3%)
  other arithmetic  6.47 us (2%)
    reduce_scatter x1, waiting for transfers between devices, on_device(): lax.psum_scatter(terms, ('grp', 'tile', 'tp'), scatter_dimension=0, tiled...  139 us
    reduce_scatter x1, waiting for transfers between devices, on_device(): lax.psum_scatter(partial_sum.astype(jnp.bfloat16), 'tp', scatter_dimensio...  40.7 us
    all_gather x1, blocking collectives, on_device(): piece = lax.all_gather(flux, 'tp', axis=0, tiled=True)  14.4 us
    ppermute x4, starting transfers between devices, _state_pages(): raw_out = lax.ppermute(raw_out, ('grp', 'tile'), copies)  9.26 us
    ppermute x4, waiting for transfers between devices, _state_pages(): raw_out = lax.ppermute(raw_out, ('grp', 'tile'), copies)  8.02 us
    ppermute x3, starting transfers between devices, _state_pages(): newest = lax.ppermute(newest, ('grp', 'tile'), row_list)  7.88 us
    dot_general x1, matrix products, on_device(): lax.dot_general(hidden, _state_pages(w_second, 0), (((1,), (1,)), ((), ()...  6.83 us
    ppermute x2, starting transfers between devices, with_halo(): lax.ppermute(lax.slice_in_dim(block, block.shape[dim] - width, None, axis...  5.97 us
  transfers between devices with their start and end apart: 14, of which 10 were waited for; matrix products, arithmetic and copies ran while one was open for 4% of the time, Pallas kernels for 0%

profile of v1, /device:TPU:0, one launch (start us, length us, event | category | flops | bytes accessed | tf_op | source)
XLA Modules:
  0.0 282.7 jit_solution(12966024250056725887)
XLA Ops:
  8.5 2.9 %collective-permute-start.1 = (bf16[192,768]{1,0:T(8,128)(2,1)}, bf16[192,768]{1,0:T(8,128)(2,1)S(1)}, u32[]{:S(2)}, u32[]{:S(2)}) collective-permute-start(bf16[192,768]{1,0:T(8,128)(2,1)} %param.17), channel_id=1, source_target_pairs={{0,28},{4,0},{8,4},{12,8},{16,12},{20,16},{24,20},{28,24},{1,29},{... | collective-permute-start | bytes 884744 | tf_op jit(solution)/shard_map/ppermute | solution.py:74
  11.4 1.8 fusion
  13.2 3.3 %collective-permute-done = bf16[192,768]{1,0:T(8,128)(2,1)S(1)} collective-permute-done((bf16[192,768]{1,0:T(8,128)(2,1)}, bf16[192,768]{1,0:T(8,128)(2,1)S(1)}, u32[]{:S(2)}, u32[]{:S(2)}) %collective-permute-start) | collective-permute-done | bytes 294944 | tf_op jit(solution)/shard_map/ppermute | solution.py:69
  17.2 0.9 collective-permute-done.1
  18.1 2.7 collective-permute-start.3
  20.8 1.6 broadcast_in_dim.2
  22.4 0.7 constant_dynamic-update-slice_fusion.7
  23.2 1.7 collective-permute-done.2
  24.8 3.7 %collective-permute-start.4 = (bf16[192,768]{1,0:T(8,128)(2,1)}, bf16[192,768]{1,0:T(8,128)(2,1)S(1)}, u32[]{:S(2)}, u32[]{:S(2)}) collective-permute-start(bf16[192,768]{1,0:T(8,128)(2,1)} %collective-permute-done.2), channel_id=1, source_target_pairs={{0,4},{4,8},{8,12},{12,16},{16,20},{20,24},{24,28},{28,0},{1,5},{5... | collective-permute-start | bytes 884744 | tf_op jit(solution)/shard_map/ppermute | solution.py:69
  28.5 0.8 constant_dynamic-update-slice_fusion.6
  29.3 0.7 constant_dynamic-update-slice_fusion.5
  30.0 2.2 collective-permute-start.5
  32.3 1.7 constant_dynamic-update-slice_fusion.4
  34.0 4.4 %collective-permute-start.6 = (bf16[192,768]{1,0:T(8,128)(2,1)S(1)}, bf16[192,768]{1,0:T(8,128)(2,1)S(1)}, u32[]{:S(2)}, u32[]{:S(2)}) collective-permute-start(bf16[192,768]{1,0:T(8,128)(2,1)S(1)} %collective-permute-done.4), channel_id=1, source_target_pairs={{0,4},{4,8},{8,12},{12,16},{16,20},{20,24},{24,28},{28,0},{1,5},{5... | collective-permute-start | bytes 884744 | tf_op jit(solution)/shard_map/ppermute | solution.py:69
  39.8 3.9 %collective-permute-done.5 = bf16[192,768]{1,0:T(8,128)(2,1)S(1)} collective-permute-done((bf16[192,768]{1,0:T(8,128)(2,1)S(1)}, bf16[192,768]{1,0:T(8,128)(2,1)S(1)}, u32[]{:S(2)}, u32[]{:S(2)}) %collective-permute-start.5) | collective-permute-done | bytes 294944 | tf_op jit(solution)/shard_map/ppermute | solution.py:74
  44.4 3.0 %collective-permute-done.6 = bf16[192,768]{1,0:T(8,128)(2,1)S(1)} collective-permute-done((bf16[192,768]{1,0:T(8,128)(2,1)S(1)}, bf16[192,768]{1,0:T(8,128)(2,1)S(1)}, u32[]{:S(2)}, u32[]{:S(2)}) %collective-permute-start.6) | collective-permute-done | bytes 294944 | tf_op jit(solution)/shard_map/ppermute | solution.py:69
  47.5 0.8 constant_dynamic-update-slice_fusion
  48.2 1.7 all-gather.2.cloned.1.call-done
  49.9 6.8 %convolution_convert_fusion = bf16[512,1536]{1,0:T(8,128)(2,1)} fusion(bf16[1536,768]{1,0:T(8,128)(2,1)} %constant_dynamic-update-slice_fusion, bf16[1536,768]{1,0:T(8,128)(2,1)} %all-gather.2.cloned.1.call-done, bf16[512,1536]{1,0:T(8,128)(2,1)S(1)} %copy-done.1, f32[1536]{0:T(1024)S(1)} %copy-done.12, f32[512]{0:T(512)S(1)} %add_rsqrt_fusion.1), kind=kOutput, calls=%fused_computation.5 | convolution fusion | flops 2423390208 | bytes 7872512 | tf_op jit(solution)/shard_map/dot_general | solution.py:80
  56.9 40.7 %reduce-scatter.3.cloned.1.call-done = bf16[128,1536]{1,0:T(8,128)(2,1)} async-done(((bf16[512,1536]{1,0:T(8,128)(2,1)}), bf16[128,1536]{1,0:T(8,128)(2,1)}) %reduce-scatter.3.cloned.1.call-update) | async-done | bytes 393232 | tf_op jit(solution)/shard_map/reduce_scatter | solution.py:89
  97.7 1.1 add_convert_fusion
  99.1 14.4 %all_gather.7 = bf16[512,256]{1,0:T(8,128)(2,1)S(1)} all-gather(bf16[128,256]{1,0:T(8,128)(2,1)S(1)} %convolution_convert_fusion.1), channel_id=1, replica_groups=mesh['grp'=2,'tile'=4,'tp'=4] {'tp'}, dimensions={0}, use_global_device_ids=true | all-gather | bytes 327680 | tf_op jit(solution)/shard_map/all_gather | solution.py:95
  114.3 1.4 collective-permute-start.7
  115.7 1.3 collective-permute-start.8
  117.1 3.4 %collective-permute-done.8 = bf16[1,32,256]{2,1,0:T(8,128)(2,1)S(1)} collective-permute-done((bf16[1,32,256]{2,1,0:T(8,128)(2,1)S(1)}, bf16[1,32,256]{2,1,0:T(8,128)(2,1)S(1)}, u32[]{:S(2)}, u32[]{:S(2)}) %collective-permute-start.8) | collective-permute-done | bytes 16416 | tf_op jit(solution)/shard_map/ppermute | solution.py:18
  120.5 1.3 collective-permute-start.10
  121.8 4.5 %collective-permute-start.9 = (bf16[10,1,256]{2,1,0:T(2,128)(2,1)S(1)}, bf16[10,1,256]{2,1,0:T(2,128)(2,1)S(1)}, u32[]{:S(2)}, u32[]{:S(2)}) collective-permute-start(bf16[10,1,256]{2,1,0:T(2,128)(2,1)S(1)} %get-tuple-element.5), channel_id=1, source_target_pairs={{0,1},{1,2},{2,3},{4,5},{5,6},{6,7},{8,9},{9,10},{10,11},{12,13},{... | collective-permute-start | bytes 15368 | tf_op jit(solution)/shard_map/ppermute | solution.py:15
  126.4 1.3 collective-permute-done.9
  129.4 3.1 %fusion.30 = f32[1024,256]{1,0:T(8,128)} fusion(bf16[256,256]{1,0:T(8,128)(2,1)S(1)} %bitcast.50, f32[256,1024]{1,0:T(8,128)S(1)} %fusion.63, bf16[256,256]{1,0:T(8,128)(2,1)S(1)} %fusion.32, bf16[1024,256]{1,0:T(8,128)(2,1)} %param.26), kind=kOutput, calls=%fused_computation.38 | convolution fusion | flops 273678336 | bytes 2883584 | tf_op jit(solution)/shard_map/dot_general | solution.py:144
  132.5 2.7 pad_maximum_fusion
  135.2 2.2 fusion.20
  137.4 138.8 %reduce-scatter.5.cloned.1.call-done = f32[64,256]{1,0:T(8,128)} async-done(((f32[2048,256]{1,0:T(8,128)}), f32[64,256]{1,0:T(8,128)}) %reduce-scatter.5.cloned.1.call-update) | async-done | bytes 65552 | tf_op jit(solution)/shard_map/reduce_scatter | solution.py:151
  (60 shorter events, 7.0 us)
Async XLA Ops:
  7.2 91.6 %copy-start = (bf16[1536,256]{1,0:T(8,128)(2,1)S(1)}, bf16[1536,256]{1,0:T(8,128)(2,1)}, u32[]{:S(2)}) copy-start(bf16[1536,256]{1,0:T(8,128)(2,1)} %param.18) | copy-start | bytes 2359300
  7.2 15.3 %copy-start.4 = (bf16[192,768]{1,0:T(8,128)(2,1)S(1)}, bf16[192,768]{1,0:T(8,128)(2,1)}, u32[]{:S(2)}) copy-start(bf16[192,768]{1,0:T(8,128)(2,1)} %param.17) | copy-start | bytes 884740
  7.2 42.7 %all-gather.2.cloned.1.call-start = ((), (), s32[]{:S(2)}) async-start(), calls=%async_computation.2 | async-start | bytes 2654208 | tf_op jit(solution)/shard_map/all_gather | solution.py:49
  7.9 89.7 %reduce-scatter.3.cloned.1.call-start = ((), (), s32[]{:S(2)}) async-start(), calls=%async_computation.3 | async-start | bytes 1966080 | tf_op jit(solution)/shard_map/reduce_scatter | solution.py:89
  8.0 8.6 %collective-permute-start = (bf16[192,768]{1,0:T(8,128)(2,1)}, bf16[192,768]{1,0:T(8,128)(2,1)S(1)}, u32[]{:S(2)}, u32[]{:S(2)}) collective-permute-start(bf16[192,768]{1,0:T(8,128)(2,1)} %param.17), channel_id=1, source_target_pairs={{0,4},{4,8},{8,12},{12,16},{16,20},{20,24},{24,28},{28,0},{1,5},{5... | collective-permute-start | bytes 884744 | tf_op jit(solution)/shard_map/ppermute | solution.py:69
  8.5 9.6 %collective-permute-start.1 = (bf16[192,768]{1,0:T(8,128)(2,1)}, bf16[192,768]{1,0:T(8,128)(2,1)S(1)}, u32[]{:S(2)}, u32[]{:S(2)}) collective-permute-start(bf16[192,768]{1,0:T(8,128)(2,1)} %param.17), channel_id=1, source_target_pairs={{0,28},{4,0},{8,4},{12,8},{16,12},{20,16},{24,20},{28,24},{1,29},{... | collective-permute-start | bytes 884744 | tf_op jit(solution)/shard_map/ppermute | solution.py:74
  16.6 8.3 %collective-permute-start.2 = (bf16[192,768]{1,0:T(8,128)(2,1)S(1)}, bf16[192,768]{1,0:T(8,128)(2,1)}, u32[]{:S(2)}, u32[]{:S(2)}) collective-permute-start(bf16[192,768]{1,0:T(8,128)(2,1)S(1)} %collective-permute-done), channel_id=1, source_target_pairs={{0,4},{4,8},{8,12},{12,16},{16,20},{20,24},{24,28},{28,0},{1,5},{5... | collective-permute-start | bytes 884744 | tf_op jit(solution)/shard_map/ppermute | solution.py:69
  18.1 11.9 %collective-permute-start.3 = (bf16[192,768]{1,0:T(8,128)(2,1)S(1)}, bf16[192,768]{1,0:T(8,128)(2,1)S(1)}, u32[]{:S(2)}, u32[]{:S(2)}) collective-permute-start(bf16[192,768]{1,0:T(8,128)(2,1)S(1)} %collective-permute-done.1), channel_id=1, source_target_pairs={{0,28},{4,0},{8,4},{12,8},{16,12},{20,16},{24,20},{28,24},{1,29},{... | collective-permute-start | bytes 884744 | tf_op jit(solution)/shard_map/ppermute | solution.py:74
  22.4 27.5 %copy-start.1 = (bf16[512,1536]{1,0:T(8,128)(2,1)S(1)}, bf16[512,1536]{1,0:T(8,128)(2,1)}, u32[]{:S(2)}) copy-start(bf16[512,1536]{1,0:T(8,128)(2,1)} %param.14) | copy-start | bytes 4718596
  22.4 27.5 %copy-start.12 = (f32[1536]{0:T(1024)S(1)}, f32[1536]{0:T(1024)}, u32[]{:S(2)}) copy-start(f32[1536]{0:T(1024)} %param.15) | copy-start | bytes 18436
  24.8 9.2 %collective-permute-start.4 = (bf16[192,768]{1,0:T(8,128)(2,1)}, bf16[192,768]{1,0:T(8,128)(2,1)S(1)}, u32[]{:S(2)}, u32[]{:S(2)}) collective-permute-start(bf16[192,768]{1,0:T(8,128)(2,1)} %collective-permute-done.2), channel_id=1, source_target_pairs={{0,4},{4,8},{8,12},{12,16},{16,20},{20,24},{24,28},{28,0},{1,5},{5... | collective-permute-start | bytes 884744 | tf_op jit(solution)/shard_map/ppermute | solution.py:69
  30.0 13.7 %collective-permute-start.5 = (bf16[192,768]{1,0:T(8,128)(2,1)S(1)}, bf16[192,768]{1,0:T(8,128)(2,1)S(1)}, u32[]{:S(2)}, u32[]{:S(2)}) collective-permute-start(bf16[192,768]{1,0:T(8,128)(2,1)S(1)} %collective-permute-done.3), channel_id=1, source_target_pairs={{0,28},{4,0},{8,4},{12,8},{16,12},{20,16},{24,20},{28,24},{1,29},{... | collective-permute-start | bytes 884744 | tf_op jit(solution)/shard_map/ppermute | solution.py:74
  34.0 13.5 %collective-permute-start.6 = (bf16[192,768]{1,0:T(8,128)(2,1)S(1)}, bf16[192,768]{1,0:T(8,128)(2,1)S(1)}, u32[]{:S(2)}, u32[]{:S(2)}) collective-permute-start(bf16[192,768]{1,0:T(8,128)(2,1)S(1)} %collective-permute-done.4), channel_id=1, source_target_pairs={{0,4},{4,8},{8,12},{12,16},{16,20},{20,24},{24,28},{28,0},{1,5},{5... | collective-permute-start | bytes 884744 | tf_op jit(solution)/shard_map/ppermute | solution.py:69
  48.2 8.6 %copy-start.8 = (s32[8,32]{1,0:T(8,128)S(1)}, s32[8,32]{1,0:T(8,128)}, u32[]{:S(2)}) copy-start(s32[8,32]{1,0:T(8,128)} %param.22) | copy-start | bytes 3076
  56.7 56.8 %copy-start.10 = (s32[2,3]{1,0:T(2,128)S(1)}, s32[2,3]{1,0:T(2,128)}, u32[]{:S(2)}) copy-start(s32[2,3]{1,0:T(2,128)} %param.19) | copy-start | bytes 76
  56.7 57.1 %copy-start.5 = (bf16[2,3,128,128]{3,2,1,0:T(8,128)(2,1)S(1)}, bf16[2,3,128,128]{3,2,1,0:T(8,128)(2,1)}, u32[]{:S(2)}) copy-start(bf16[2,3,128,128]{3,2,1,0:T(8,128)(2,1)} %param.20) | copy-start | bytes 589828
  56.8 57.4 %copy-start.7 = (bf16[8,32,256]{2,1,0:T(8,128)(2,1)S(1)}, bf16[8,32,256]{2,1,0:T(8,128)(2,1)}, u32[]{:S(2)}) copy-start(bf16[8,32,256]{2,1,0:T(8,128)(2,1)} %param.21) | copy-start | bytes 393220
  56.8 219.4 %reduce-scatter.5.cloned.1.call-start = ((), (), s32[]{:S(2)}) async-start(), calls=%async_computation.4 | async-start | bytes 2162688 | tf_op jit(solution)/shard_map/reduce_scatter | solution.py:151
  56.9 60.1 %copy-start.6 = (bf16[8,32,256]{2,1,0:T(8,128)(2,1)S(1)}, bf16[8,32,256]{2,1,0:T(8,128)(2,1)}, u32[]{:S(2)}) copy-start(bf16[8,32,256]{2,1,0:T(8,128)(2,1)} %param.27) | copy-start | bytes 393220
  98.8 29.0 %copy-start.2 = (bf16[128,1536]{1,0:T(8,128)(2,1)}, bf16[128,1536]{1,0:T(8,128)(2,1)S(1)}, u32[]{:S(2)}) copy-start(bf16[128,1536]{1,0:T(8,128)(2,1)S(1)} %add_convert_fusion) | copy-start | bytes 1179652
  98.8 27.6 %copy-start.9 = (f32[3,3,256]{2,1,0:T(4,128)S(1)}, f32[3,3,256]{2,1,0:T(4,128)}, u32[]{:S(2)}) copy-start(f32[3,3,256]{2,1,0:T(4,128)} %param.23) | copy-start | bytes 27652
  114.1 14.2 %copy-start.11 = (f32[256]{0:T(256)S(1)}, f32[256]{0:T(256)}, u32[]{:S(2)}) copy-start(f32[256]{0:T(256)} %param.24) | copy-start | bytes 3076
  114.2 14.2 %copy-start.3 = (bf16[256,1024]{1,0:T(8,128)(2,1)S(1)}, bf16[256,1024]{1,0:T(8,128)(2,1)}, u32[]{:S(2)}) copy-start(bf16[256,1024]{1,0:T(8,128)(2,1)} %param.25) | copy-start | bytes 1572868
  114.3 2.9 %collective-permute-start.7 = (bf16[1,32,256]{2,1,0:T(8,128)(2,1)S(1)}, bf16[1,32,256]{2,1,0:T(8,128)(2,1)S(1)}, u32[]{:S(2)}, u32[]{:S(2)}) collective-permute-start(bf16[1,32,256]{2,1,0:T(8,128)(2,1)S(1)} %get-tuple-element.7), channel_id=1, source_target_pairs={{0,4},{4,8},{8,12},{12,16},{16,20},{20,24},{24,28},{1,5},{5,9},{9,... | collective-permute-start | bytes 49160 | tf_op jit(solution)/shard_map/ppermute | solution.py:15
  115.7 4.8 %collective-permute-start.8 = (bf16[1,32,256]{2,1,0:T(8,128)(2,1)S(1)}, bf16[1,32,256]{2,1,0:T(8,128)(2,1)S(1)}, u32[]{:S(2)}, u32[]{:S(2)}) collective-permute-start(bf16[1,32,256]{2,1,0:T(8,128)(2,1)S(1)} %get-tuple-element.8), channel_id=1, source_target_pairs={{4,0},{8,4},{12,8},{16,12},{20,16},{24,20},{28,24},{5,1},{9,5},{13... | collective-permute-start | bytes 49160 | tf_op jit(solution)/shard_map/ppermute | solution.py:18
  120.5 5.9 %collective-permute-start.10 = (bf16[10,1,256]{2,1,0:T(2,128)(2,1)S(1)}, bf16[10,1,256]{2,1,0:T(2,128)(2,1)S(1)}, u32[]{:S(2)}, u32[]{:S(2)}) collective-permute-start(bf16[10,1,256]{2,1,0:T(2,128)(2,1)S(1)} %get-tuple-element.6), channel_id=1, source_target_pairs={{1,0},{2,1},{3,2},{5,4},{6,5},{7,6},{9,8},{10,9},{11,10},{13,12},{... | collective-permute-start | bytes 15368 | tf_op jit(solution)/shard_map/ppermute | solution.py:18
  121.8 5.9 %collective-permute-start.9 = (bf16[10,1,256]{2,1,0:T(2,128)(2,1)S(1)}, bf16[10,1,256]{2,1,0:T(2,128)(2,1)S(1)}, u32[]{:S(2)}, u32[]{:S(2)}) collective-permute-start(bf16[10,1,256]{2,1,0:T(2,128)(2,1)S(1)} %get-tuple-element.5), channel_id=1, source_target_pairs={{0,1},{1,2},{2,3},{4,5},{5,6},{6,7},{8,9},{9,10},{10,11},{12,13},{... | collective-permute-start | bytes 15368 | tf_op jit(solution)/shard_map/ppermute | solution.py:15
Sparse Core Ops, SparseCore 0:
  9.9 39.9 all-gather.1
  56.9 40.7 reduce-scatter.2
  135.3 140.8 reduce-scatter.4
